TPU v7x, 128 devices: a whole 4x4x4 slice. The times are simulated.
128 devices in a mesh: parts: 128 (over y, z, x, core).
Axes of the slice: x: 4, y: 4, z: 4, core: 2. Of those that a mesh axis runs over, the one named last changes fastest.
Arguments:
- rhs: float32 [4, 131072], P(None, 'parts'), may hold values from -6 to 6
- diag_tiles: bfloat16 [1024, 512, 512], P('parts'), may hold values from -1 to 6, as said below
- local_tiles: bfloat16 [1024, 3, 512, 512], P('parts'), may hold values from -0.125 to 0.125
- up_tiles: bfloat16 [384, 512, 512], P('parts'), may hold values from -0.375 to 0.375
- down_tiles: bfloat16 [384, 512, 512], P('parts'), may hold values from -0.375 to 0.375
- pattern: int32 [1024, 3], P('parts'), may hold values from 0 to 7
- coupling_rows: int32 [128, 6], P('parts'), may hold values from 0 to 7
- ghost_rows: int32 [128, 6, 128], P('parts'), may hold values from 0 to 1023
- pair_live: int32 [128, 3], P('parts'), may hold values 0 or 1
Outputs:
- adjoint: float32 [4, 131072], P(None, 'parts')
Inputs may be any that keep to these rules, and one draw needn't show every extreme that they name: `diag_tiles`: each tile is its own diagonal entries of 0.5 to 5 plus a dense remainder of smaller entries.
All inputs are finite; a program needn't handle non-finite values. No bound on the sum of `pair_live` on one device may be relied on, other than what follows from the above.
Results may differ from a plain program's by a relative error of at most 0.0028.
Values may be sent and summed in bfloat16 or wider, within the bound.
A program may use at most 128 MiB of HBM per device.

v0:
```python
import jax
import jax.numpy as jnp
from jax import lax
from jax.sharding import PartitionSpec as P

COMP = 4
TILE = 128
TD = 8
W = 3
ITERS = 3


def from_behind(value, axis, steps):
    count = lax.axis_size(axis)
    pairs = [(source, (source + steps) % count) for source in range(count)]
    return lax.ppermute(value, axis, pairs)


def local(
    rhs,
    diag_tiles,
    local_tiles,
    up_tiles,
    down_tiles,
    pattern,
    coupling_rows,
    ghost_rows,
    pair_live,
):
    width = COMP * TILE
    own_live = pair_live[0].astype(jnp.float32)
    row_tiles = coupling_rows[0]
    ghosts = ghost_rows[0]
    onehot = (pattern[:, :, None] == jnp.arange(TD, dtype=jnp.int32)[None, None, :]).astype(
        jnp.float32
    )
    ghost_up_in = []
    live_in = []
    ghost_down_in = []
    tiles_up_in = []
    tiles_down_in = []
    for slot in range(W):
        offset = slot + 1
        got_ghost, got_live = from_behind((ghosts[slot], pair_live[0, slot]), "parts", offset)
        ghost_up_in.append(got_ghost)
        live_in.append(got_live.astype(jnp.float32))
        ghost_down_in.append(from_behind(ghosts[W + slot], "parts", -offset))
        tiles_up_in.append(from_behind(up_tiles[slot], "parts", offset))
        tiles_down_in.append(from_behind(down_tiles[slot], "parts", -offset))
    beta = jnp.sqrt(lax.psum(jnp.sum(rhs * rhs), "parts") + 1e-06)
    basis = [rhs / beta]
    hess = jnp.zeros((ITERS + 1, ITERS), jnp.float32)
    for j in range(ITERS):
        tiles = (
            basis[j]
            .reshape(COMP, TD, TILE)
            .transpose(1, 0, 2)
            .reshape(TD, width)
            .astype(jnp.bfloat16)
        )
        own = jnp.einsum("tr,trc->tc", tiles, diag_tiles, preferred_element_type=jnp.float32)
        mixed = jnp.einsum("tr,tkrc->tkc", tiles, local_tiles, preferred_element_type=jnp.float32)
        own = own + jnp.einsum("tkj,tkc->jc", onehot, mixed)
        result = own.reshape(TD, COMP, TILE).transpose(1, 0, 2).reshape(COMP, TD * TILE)
        for apply_slot in range(W):
            apply_offset = apply_slot + 1
            got_up = from_behind(tiles[row_tiles[apply_slot]], "parts", apply_offset)
            term_up = (
                jnp.dot(got_up, tiles_up_in[apply_slot], preferred_element_type=jnp.float32)
                * live_in[apply_slot]
            )
            got_down = from_behind(tiles[row_tiles[W + apply_slot]], "parts", -apply_offset)
            term_down = (
                jnp.dot(got_down, tiles_down_in[apply_slot], preferred_element_type=jnp.float32)
                * own_live[apply_slot]
            )
            result = result.at[:, ghost_up_in[apply_slot]].add(term_up.reshape(COMP, TILE))
            result = result.at[:, ghost_down_in[apply_slot]].add(term_down.reshape(COMP, TILE))
        vector = result
        for i in range(j + 1):
            coeff = lax.psum(jnp.sum(vector * basis[i]), "parts")
            hess = hess.at[i, j].set(coeff)
            vector = vector - coeff * basis[i]
        squared = lax.psum(jnp.sum(vector * vector), "parts")
        scale = jnp.sqrt(squared + 1e-06)
        hess = hess.at[j + 1, j].set(scale)
        if j + 1 < ITERS:
            basis.append(vector / scale)
    gram = jnp.dot(hess.T, hess, precision=lax.Precision.HIGHEST)
    target = beta * hess[0, :]
    factor = jnp.linalg.cholesky(gram)
    inner = lax.linalg.triangular_solve(factor, target[:, None], left_side=True, lower=True)
    weights = lax.linalg.triangular_solve(
        factor, inner, left_side=True, lower=True, transpose_a=True
    )[:, 0]
    adjoint = jnp.zeros_like(rhs)
    for j in range(ITERS):
        adjoint = adjoint + weights[j] * basis[j]
    return adjoint


def solution(mesh):
    in_specs = (
        P(None, "parts"),
        P("parts", None, None),
        P("parts", None, None, None),
        P("parts", None, None),
        P("parts", None, None),
        P("parts", None),
        P("parts", None),
        P("parts", None, None),
        P("parts", None),
    )
    out_specs = P(None, "parts")
    return jax.shard_map(local, mesh=mesh, in_specs=in_specs, out_specs=out_specs, check_vma=False)
```

profile of v0, /device:TPU:1, one launch (start us, length us, event | category | flops | bytes accessed | tf_op | source)
XLA Modules:
  0.0 940.2 jit_solution(1958760557065666879)
XLA Ops:
  13.7 66.6 %psum.70 = f32[]{:T(128)} all-reduce(f32[]{:T(128)} %multiply_reduce_fusion.9), channel_id=1, replica_groups=mesh['parts'=128] {'parts'}, use_global_device_ids=true, to_apply=%region_1.0 | all-reduce | flops 1 | bytes 8 | tf_op jit(solution)/shard_map/psum | solution.py:50
  92.6 6.4 fusion.20
  112.6 8.4 collective-permute-done.17
  121.0 8.4 collective-permute-start.5
  131.1 6.7 collective-permute-done.7
  140.8 8.0 collective-permute-done.14
  154.3 6.4 collective-permute-start.12
  160.7 7.2 collective-permute-start.19
  175.4 7.3 collective-permute-start.20
  189.1 8.2 collective-permute-done.13
  227.6 64.2 %psum.71 = f32[]{:T(128)} all-reduce(f32[]{:T(128)} %multiply_reduce_fusion.8), channel_id=1, replica_groups=mesh['parts'=128] {'parts'}, use_global_device_ids=true, to_apply=%region_9.0 | all-reduce | flops 1 | bytes 8 | tf_op jit(solution)/shard_map/psum | solution.py:81
  293.7 64.4 %psum.72 = f32[]{:T(128)} all-reduce(f32[]{:T(128)} %multiply_reduce_fusion.7), channel_id=1, replica_groups=mesh['parts'=128] {'parts'}, use_global_device_ids=true, to_apply=%region_11.0 | all-reduce | flops 1 | bytes 8 | tf_op jit(solution)/shard_map/psum | solution.py:84
  359.6 6.5 fusion.16
  376.1 7.4 collective-permute-start.26
  408.9 70.9 %psum.73 = f32[]{:T(128)} all-reduce(f32[]{:T(128)} %multiply_reduce_fusion.6), channel_id=1, replica_groups=mesh['parts'=128] {'parts'}, use_global_device_ids=true, to_apply=%region_19.0 | all-reduce | flops 1 | bytes 8 | tf_op jit(solution)/shard_map/psum | solution.py:81
  481.1 64.2 %psum.74 = f32[]{:T(128)} all-reduce(f32[]{:T(128)} %multiply_reduce_fusion.5), channel_id=1, replica_groups=mesh['parts'=128] {'parts'}, use_global_device_ids=true, to_apply=%region_21.0 | all-reduce | flops 1 | bytes 8 | tf_op jit(solution)/shard_map/psum | solution.py:81
  547.2 62.5 %psum.75 = f32[]{:T(128)} all-reduce(f32[]{:T(128)} %get-tuple-element.133), channel_id=1, replica_groups=mesh['parts'=128] {'parts'}, use_global_device_ids=true, to_apply=%region_23.0 | all-reduce | flops 1 | bytes 8 | tf_op jit(solution)/shard_map/psum | solution.py:84
  610.5 6.5 fusion.12
  621.2 6.8 collective-permute-start.30
  630.7 7.2 collective-permute-start.32
  661.8 69.6 %psum.76 = f32[]{:T(128)} all-reduce(f32[]{:T(128)} %multiply_reduce_fusion.3), channel_id=1, replica_groups=mesh['parts'=128] {'parts'}, use_global_device_ids=true, to_apply=%region_32.0 | all-reduce | flops 1 | bytes 8 | tf_op jit(solution)/shard_map/psum | solution.py:81
  734.7 64.2 %psum.77 = f32[]{:T(128)} all-reduce(f32[]{:T(128)} %multiply_reduce_fusion.2), channel_id=1, replica_groups=mesh['parts'=128] {'parts'}, use_global_device_ids=true, to_apply=%region_34.0 | all-reduce | flops 1 | bytes 8 | tf_op jit(solution)/shard_map/psum | solution.py:81
  800.8 62.5 %psum.78 = f32[]{:T(128)} all-reduce(f32[]{:T(128)} %get-tuple-element.131), channel_id=1, replica_groups=mesh['parts'=128] {'parts'}, use_global_device_ids=true, to_apply=%region_36.0 | all-reduce | flops 1 | bytes 8 | tf_op jit(solution)/shard_map/psum | solution.py:81
  867.7 64.1 %psum.79 = f32[]{:T(128)} all-reduce(f32[]{:T(128)} %multiply_reduce_fusion), channel_id=1, replica_groups=mesh['parts'=128] {'parts'}, use_global_device_ids=true, to_apply=%region_38.0 | all-reduce | flops 1 | bytes 8 | tf_op jit(solution)/shard_map/psum | solution.py:84
  (242 shorter events, 166.8 us)
Async XLA Ops:
  0.7 129.2 %collective-permute-start = (s32[128]{0:T(128)S(1)}, s32[128]{0:T(128)S(1)}, u32[]{:S(2)}, u32[]{:S(2)}) collective-permute-start(s32[128]{0:T(128)S(1)} %get-tuple-element.158), channel_id=1, source_target_pairs={{0,1},{1,2},{2,3},{3,4},{4,5},{5,6},{6,7},{7,8},{8,9},{9,10},{10,1... | collective-permute-start | bytes 1544 | tf_op jit(solution)/shard_map/ppermute | solution.py:16
  85.6 68.7 %collective-permute-start.1 = (bf16[512]{0:T(512)(128)(2,1)S(1)}, bf16[512]{0:T(512)(128)(2,1)S(1)}, u32[]{:S(2)}, u32[]{:S(2)}) collective-permute-start(bf16[512]{0:T(512)(128)(2,1)S(1)} %get-tuple-element.129), channel_id=1, source_target_pairs={{0,1},{1,2},{2,3},{3,4},{4,5},{5,6},{6,7},{7,8},{8,9},{9,10},{10,1... | collective-permute-start | bytes 3080 | tf_op jit(solution)/shard_map/ppermute | solution.py:16
  89.9 85.5 %collective-permute-start.2 = (bf16[512,512]{1,0:T(8,128)(2,1)}, bf16[512,512]{1,0:T(8,128)(2,1)S(1)}, u32[]{:S(2)}, u32[]{:S(2)}) collective-permute-start(bf16[512,512]{1,0:T(8,128)(2,1)} %get-tuple-element.143), channel_id=1, source_target_pairs={{0,1},{1,2},{2,3},{3,4},{4,5},{5,6},{6,7},{7,8},{8,9},{9,10},{10,1... | collective-permute-start | bytes 1572872 | tf_op jit(solution)/shard_map/ppermute | solution.py:16
  91.2 12.9 %collective-permute-start.3 = (s32[]{:T(128)}, s32[]{:T(128)}, u32[]{:S(2)}, u32[]{:S(2)}) collective-permute-start(s32[]{:T(128)} %bitcast.15), channel_id=1, source_target_pairs={{0,1},{1,2},{2,3},{3,4},{4,5},{5,6},{6,7},{7,8},{8,9},{9,10},{10,1... | collective-permute-start | bytes 20 | tf_op jit(solution)/shard_map/ppermute | solution.py:16
  91.9 38.6 %collective-permute-start.4 = (s32[128]{0:T(128)S(1)}, s32[128]{0:T(128)S(1)}, u32[]{:S(2)}, u32[]{:S(2)}) collective-permute-start(s32[128]{0:T(128)S(1)} %get-tuple-element.157), channel_id=1, source_target_pairs={{0,127},{1,0},{2,1},{3,2},{4,3},{5,4},{6,5},{7,6},{8,7},{9,8},{10,... | collective-permute-start | bytes 1544 | tf_op jit(solution)/shard_map/ppermute | solution.py:16
  121.0 39.7 %collective-permute-start.5 = (bf16[512]{0:T(512)(128)(2,1)S(1)}, bf16[512]{0:T(512)(128)(2,1)S(1)}, u32[]{:S(2)}, u32[]{:S(2)}) collective-permute-start(bf16[512]{0:T(512)(128)(2,1)S(1)} %get-tuple-element.128), channel_id=1, source_target_pairs={{0,127},{1,0},{2,1},{3,2},{4,3},{5,4},{6,5},{7,6},{8,7},{9,8},{10,... | collective-permute-start | bytes 3080 | tf_op jit(solution)/shard_map/ppermute | solution.py:16
  130.5 30.1 %collective-permute-start.8 = (bf16[512]{0:T(512)(128)(2,1)S(1)}, bf16[512]{0:T(512)(128)(2,1)S(1)}, u32[]{:S(2)}, u32[]{:S(2)}) collective-permute-start(bf16[512]{0:T(512)(128)(2,1)S(1)} %get-tuple-element.127), channel_id=1, source_target_pairs={{0,2},{1,3},{2,4},{3,5},{4,6},{5,7},{6,8},{7,9},{8,10},{9,11},{10,... | collective-permute-start | bytes 3080 | tf_op jit(solution)/shard_map/ppermute | solution.py:16
  153.4 29.5 %collective-permute-start.6 = (bf16[512,512]{1,0:T(8,128)(2,1)}, bf16[512,512]{1,0:T(8,128)(2,1)S(1)}, u32[]{:S(2)}, u32[]{:S(2)}) collective-permute-start(bf16[512,512]{1,0:T(8,128)(2,1)} %get-tuple-element.140), channel_id=1, source_target_pairs={{0,127},{1,0},{2,1},{3,2},{4,3},{5,4},{6,5},{7,6},{8,7},{9,8},{10,... | collective-permute-start | bytes 1572872 | tf_op jit(solution)/shard_map/ppermute | solution.py:16
  154.3 14.0 %collective-permute-start.12 = (bf16[512]{0:T(512)(128)(2,1)S(1)}, bf16[512]{0:T(512)(128)(2,1)S(1)}, u32[]{:S(2)}, u32[]{:S(2)}) collective-permute-start(bf16[512]{0:T(512)(128)(2,1)S(1)} %get-tuple-element.126), channel_id=1, source_target_pairs={{0,126},{1,127},{2,0},{3,1},{4,2},{5,3},{6,4},{7,5},{8,6},{9,7},{1... | collective-permute-start | bytes 3080 | tf_op jit(solution)/shard_map/ppermute | solution.py:16
  160.7 14.7 %collective-permute-start.19 = (bf16[512]{0:T(512)(128)(2,1)S(1)}, bf16[512]{0:T(512)(128)(2,1)S(1)}, u32[]{:S(2)}, u32[]{:S(2)}) collective-permute-start(bf16[512]{0:T(512)(128)(2,1)S(1)} %get-tuple-element.125), channel_id=1, source_target_pairs={{0,125},{1,126},{2,127},{3,0},{4,1},{5,2},{6,3},{7,4},{8,5},{9,6},... | collective-permute-start | bytes 3080 | tf_op jit(solution)/shard_map/ppermute | solution.py:16
  168.3 20.6 %collective-permute-start.9 = (bf16[512,512]{1,0:T(8,128)(2,1)}, bf16[512,512]{1,0:T(8,128)(2,1)S(1)}, u32[]{:S(2)}, u32[]{:S(2)}) collective-permute-start(bf16[512,512]{1,0:T(8,128)(2,1)} %get-tuple-element.144), channel_id=1, source_target_pairs={{0,2},{1,3},{2,4},{3,5},{4,6},{5,7},{6,8},{7,9},{8,10},{9,11},{10,... | collective-permute-start | bytes 1572872 | tf_op jit(solution)/shard_map/ppermute | solution.py:16
  169.3 28.0 %collective-permute-start.13 = (bf16[512,512]{1,0:T(8,128)(2,1)}, bf16[512,512]{1,0:T(8,128)(2,1)S(1)}, u32[]{:S(2)}, u32[]{:S(2)}) collective-permute-start(bf16[512,512]{1,0:T(8,128)(2,1)} %get-tuple-element.141), channel_id=1, source_target_pairs={{0,126},{1,127},{2,0},{3,1},{4,2},{5,3},{6,4},{7,5},{8,6},{9,7},{1... | collective-permute-start | bytes 1572872 | tf_op jit(solution)/shard_map/ppermute | solution.py:16
  175.3 29.2 %collective-permute-start.16 = (bf16[512,512]{1,0:T(8,128)(2,1)}, bf16[512,512]{1,0:T(8,128)(2,1)S(1)}, u32[]{:S(2)}, u32[]{:S(2)}) collective-permute-start(bf16[512,512]{1,0:T(8,128)(2,1)} %get-tuple-element.142), channel_id=1, source_target_pairs={{0,3},{1,4},{2,5},{3,6},{4,7},{5,8},{6,9},{7,10},{8,11},{9,12},{10... | collective-permute-start | bytes 1572872 | tf_op jit(solution)/shard_map/ppermute | solution.py:16
  175.4 29.5 %collective-permute-start.20 = (bf16[512,512]{1,0:T(8,128)(2,1)}, bf16[512,512]{1,0:T(8,128)(2,1)S(1)}, u32[]{:S(2)}, u32[]{:S(2)}) collective-permute-start(bf16[512,512]{1,0:T(8,128)(2,1)} %get-tuple-element.139), channel_id=1, source_target_pairs={{0,125},{1,126},{2,127},{3,0},{4,1},{5,2},{6,3},{7,4},{8,5},{9,6},... | collective-permute-start | bytes 1572872 | tf_op jit(solution)/shard_map/ppermute | solution.py:16
  368.1 15.6 %collective-permute-start.22 = (bf16[512]{0:T(512)(128)(2,1)S(1)}, bf16[512]{0:T(512)(128)(2,1)S(1)}, u32[]{:S(2)}, u32[]{:S(2)}) collective-permute-start(bf16[512]{0:T(512)(128)(2,1)S(1)} %get-tuple-element.122), channel_id=1, source_target_pairs={{0,127},{1,0},{2,1},{3,2},{4,3},{5,4},{6,5},{7,6},{8,7},{9,8},{10,... | collective-permute-start | bytes 3080 | tf_op jit(solution)/shard_map/ppermute | solution.py:16
  369.2 15.3 %collective-permute-start.23 = (bf16[512]{0:T(512)(128)(2,1)S(1)}, bf16[512]{0:T(512)(128)(2,1)S(1)}, u32[]{:S(2)}, u32[]{:S(2)}) collective-permute-start(bf16[512]{0:T(512)(128)(2,1)S(1)} %get-tuple-element.121), channel_id=1, source_target_pairs={{0,2},{1,3},{2,4},{3,5},{4,6},{5,7},{6,8},{7,9},{8,10},{9,11},{10,... | collective-permute-start | bytes 3080 | tf_op jit(solution)/shard_map/ppermute | solution.py:16
  369.8 14.9 %collective-permute-start.24 = (bf16[512]{0:T(512)(128)(2,1)S(1)}, bf16[512]{0:T(512)(128)(2,1)S(1)}, u32[]{:S(2)}, u32[]{:S(2)}) collective-permute-start(bf16[512]{0:T(512)(128)(2,1)S(1)} %get-tuple-element.120), channel_id=1, source_target_pairs={{0,126},{1,127},{2,0},{3,1},{4,2},{5,3},{6,4},{7,5},{8,6},{9,7},{1... | collective-permute-start | bytes 3080 | tf_op jit(solution)/shard_map/ppermute | solution.py:16
  376.1 10.2 %collective-permute-start.26 = (bf16[512]{0:T(512)(128)(2,1)S(1)}, bf16[512]{0:T(512)(128)(2,1)S(1)}, u32[]{:S(2)}, u32[]{:S(2)}) collective-permute-start(bf16[512]{0:T(512)(128)(2,1)S(1)} %get-tuple-element.119), channel_id=1, source_target_pairs={{0,125},{1,126},{2,127},{3,0},{4,1},{5,2},{6,3},{7,4},{8,5},{9,6},... | collective-permute-start | bytes 3080 | tf_op jit(solution)/shard_map/ppermute | solution.py:16
  617.6 13.1 %collective-permute-start.27 = (bf16[512]{0:T(512)(128)(2,1)S(1)}, bf16[512]{0:T(512)(128)(2,1)S(1)}, u32[]{:S(2)}, u32[]{:S(2)}) collective-permute-start(bf16[512]{0:T(512)(128)(2,1)S(1)} %get-tuple-element.117), channel_id=1, source_target_pairs={{0,1},{1,2},{2,3},{3,4},{4,5},{5,6},{6,7},{7,8},{8,9},{9,10},{10,1... | collective-permute-start | bytes 3080 | tf_op jit(solution)/shard_map/ppermute | solution.py:16
  621.1 17.1 %collective-permute-start.28 = (bf16[512]{0:T(512)(128)(2,1)S(1)}, bf16[512]{0:T(512)(128)(2,1)S(1)}, u32[]{:S(2)}, u32[]{:S(2)}) collective-permute-start(bf16[512]{0:T(512)(128)(2,1)S(1)} %get-tuple-element.116), channel_id=1, source_target_pairs={{0,127},{1,0},{2,1},{3,2},{4,3},{5,4},{6,5},{7,6},{8,7},{9,8},{10,... | collective-permute-start | bytes 3080 | tf_op jit(solution)/shard_map/ppermute | solution.py:16
  621.1 17.9 %collective-permute-start.29 = (bf16[512]{0:T(512)(128)(2,1)S(1)}, bf16[512]{0:T(512)(128)(2,1)S(1)}, u32[]{:S(2)}, u32[]{:S(2)}) collective-permute-start(bf16[512]{0:T(512)(128)(2,1)S(1)} %get-tuple-element.115), channel_id=1, source_target_pairs={{0,2},{1,3},{2,4},{3,5},{4,6},{5,7},{6,8},{7,9},{8,10},{9,11},{10,... | collective-permute-start | bytes 3080 | tf_op jit(solution)/shard_map/ppermute | solution.py:16
  621.2 18.0 %collective-permute-start.30 = (bf16[512]{0:T(512)(128)(2,1)S(1)}, bf16[512]{0:T(512)(128)(2,1)S(1)}, u32[]{:S(2)}, u32[]{:S(2)}) collective-permute-start(bf16[512]{0:T(512)(128)(2,1)S(1)} %get-tuple-element.114), channel_id=1, source_target_pairs={{0,126},{1,127},{2,0},{3,1},{4,2},{5,3},{6,4},{7,5},{8,6},{9,7},{1... | collective-permute-start | bytes 3080 | tf_op jit(solution)/shard_map/ppermute | solution.py:16
  628.0 12.1 %collective-permute-start.31 = (bf16[512]{0:T(512)(128)(2,1)S(1)}, bf16[512]{0:T(512)(128)(2,1)S(1)}, u32[]{:S(2)}, u32[]{:S(2)}) collective-permute-start(bf16[512]{0:T(512)(128)(2,1)S(1)} %get-tuple-element.118), channel_id=1, source_target_pairs={{0,3},{1,4},{2,5},{3,6},{4,7},{5,8},{6,9},{7,10},{8,11},{9,12},{10... | collective-permute-start | bytes 3080 | tf_op jit(solution)/shard_map/ppermute | solution.py:16
  630.7 10.1 %collective-permute-start.32 = (bf16[512]{0:T(512)(128)(2,1)S(1)}, bf16[512]{0:T(512)(128)(2,1)S(1)}, u32[]{:S(2)}, u32[]{:S(2)}) collective-permute-start(bf16[512]{0:T(512)(128)(2,1)S(1)} %get-tuple-element.113), channel_id=1, source_target_pairs={{0,125},{1,126},{2,127},{3,0},{4,1},{5,2},{6,3},{7,4},{8,5},{9,6},... | collective-permute-start | bytes 3080 | tf_op jit(solution)/shard_map/ppermute | solution.py:16
  (22 other events, 271.7 us)
where the time goes:
time: 951 us; the launch traced here: 940 us
  blocking collectives  653 us (69%)
  other arithmetic  84.2 us (9%)
  starting transfers between devices  77.8 us (8%)
  waiting for transfers between devices  52 us (5%)
  local copies, waits for them, and re-layouts  28.8 us (3%)
  matrix products  25.4 us (3%)
  between operations  18.7 us (2%)
    psum x6, blocking collectives, local(): coeff = lax.psum(jnp.sum(vector * basis[i]), 'parts')  396 us
    psum x3, blocking collectives, local(): squared = lax.psum(jnp.sum(vector * vector), 'parts')  191 us
    ppermute x33, starting transfers between devices, from_behind(): return lax.ppermute(value, axis, pairs)  77.8 us
    psum x1, blocking collectives, local(): beta = jnp.sqrt(lax.psum(jnp.sum(rhs * rhs), 'parts') + 1e-06)  66.6 us
    ppermute x33, waiting for transfers between devices, from_behind(): return lax.ppermute(value, axis, pairs)  52 us
    scatter-add x9, other arithmetic, local(): result.at[:, ghost_down_in[apply_slot]].add(term_down.reshape(COMP, TILE))  27.7 us
    scatter-add x9, other arithmetic, local(): result.at[:, ghost_up_in[apply_slot]].add(term_up.reshape(COMP, TILE))  27.3 us
    dot_general x3, matrix products, local(): jnp.einsum('tr,tkrc->tkc', tiles, local_tiles, preferred_element_type=jnp...  19.3 us
  transfers between devices with their start and end apart: 33, of which 10 were waited for; matrix products, arithmetic and copies ran while one was open for 4% of the time, Pallas kernels for 0%

commit v1 on v0

v1 whole, which is shorter than its diff:
```python
import functools

import jax
import jax.numpy as jnp
from jax import lax
from jax.experimental import pallas as pl
from jax.experimental.pallas import tpu as pltpu
from jax.sharding import PartitionSpec as P

COMP = 4
TILE = 128
TD = 8
KL = 3
W = 3
ITERS = 3
WIDTH = COMP * TILE
SLOTS = 2 * W
PER_ROW = KL + 1
SHIFT = 2.0
EPS = 1e-06
ROW = 8
MESH = pl.DeviceIdType.MESH
F32 = jnp.float32
BF16 = jnp.bfloat16
PAIRS = [(i, j) for i in range(ITERS + 1) for j in range(i, ITERS + 1)]


def lanes(c):
    return slice(c * TILE, (c + 1) * TILE)


def halves(x):
    high = x.astype(BF16).astype(F32)
    return jnp.concatenate([high, x - high], axis=0).astype(BF16)


def small_solve(gram):
    n = ITERS + 1

    def g(i, j):
        return gram[(min(i, j), max(i, j))]

    def dot(u, v):
        total = None
        for i, a in u.items():
            for j, b in v.items():
                term = a * b * g(i, j)
                total = term if total is None else total + term
        return total

    beta = jnp.sqrt(g(0, 0) + EPS)
    basis = [{0: 1.0 / beta}]
    hess = {}
    for j in range(ITERS):
        w = {}
        for i, a in basis[j].items():
            w[i + 1] = a + w[i + 1] if i + 1 in w else a
            w[i] = SHIFT * a + w[i] if i in w else SHIFT * a
        for i in range(j + 1):
            hess[i, j] = dot(w, basis[i])
            for k, b in basis[i].items():
                w[k] = w[k] - hess[i, j] * b
        scale = jnp.sqrt(jnp.maximum(dot(w, w), 0.0) + EPS)
        hess[j + 1, j] = scale
        if j + 1 < ITERS:
            inverse = 1.0 / scale
            basis.append({k: a * inverse for k, a in w.items()})
    normal = {}
    for a in range(ITERS):
        for b in range(a + 1):
            normal[a, b] = sum(
                hess[i, a] * hess[i, b] for i in range(n) if (i, a) in hess and (i, b) in hess
            )
    target = [beta * hess[0, j] for j in range(ITERS)]
    low = {}
    inv = []
    for a in range(ITERS):
        for b in range(a):
            value = normal[a, b]
            for k in range(b):
                value = value - low[a, k] * low[b, k]
            low[a, b] = value * inv[b]
        value = normal[a, a]
        for k in range(a):
            value = value - low[a, k] * low[a, k]
        inv.append(1.0 / jnp.sqrt(value))
    inner = []
    for a in range(ITERS):
        value = target[a]
        for k in range(a):
            value = value - low[a, k] * inner[k]
        inner.append(value * inv[a])
    weights = [None] * ITERS
    for a in reversed(range(ITERS)):
        value = inner[a]
        for k in range(a + 1, ITERS):
            value = value - low[k, a] * weights[k]
        weights[a] = value * inv[a]
    out = []
    for i in range(ITERS):
        out.append(sum(weights[j] * basis[j][i] for j in range(ITERS) if i in basis[j]))
    return out


def kernel(
    n,
    rhs_hbm,
    diag_hbm,
    local_hbm,
    up_hbm,
    down_hbm,
    pattern,
    rows,
    ghost_hbm,
    live,
    out_ref,
    tiles,
    rhs,
    krylov,
    nodes,
    spread,
    masks,
    ghosts,
    pick,
    place,
    sent,
    got,
    part_a,
    part_b,
    recv_a,
    recv_b,
    load_sem,
    ghost_send,
    ghost_recv,
    halo_send,
    halo_recv,
    send_a,
    got_a,
    send_b,
    got_b,
):
    me = lax.axis_index("parts")
    columns = n // ROW
    place_in_row = lax.rem(me, ROW)
    base = me - place_in_row
    around = [lax.rem(me + s + 1, n) for s in range(W)] + [
        lax.rem(me + n - s - 1, n) for s in range(W)
    ]
    peers_a = [base + lax.rem(place_in_row + d, ROW) for d in range(1, ROW)]
    peers_b = [lax.rem(me + d * ROW, n) for d in range(1, columns)]
    everyone = around + peers_a + peers_b
    barrier = pltpu.get_barrier_semaphore()
    for other in everyone:
        pl.semaphore_signal(barrier, inc=1, device_id=(other,), device_id_type=MESH)

    loads = []

    def load(source, target):
        copy = pltpu.make_async_copy(source, target, load_sem.at[len(loads)])
        copy.start()
        loads.append(copy)
        return copy

    load_rhs = load(rhs_hbm, rhs)
    load_up = load(up_hbm, tiles.at[pl.ds(0, W)])
    load_down = load(down_hbm, tiles.at[pl.ds(W, W)])
    load_rows = []
    for t in range(TD):
        first = SLOTS + PER_ROW * t
        load_rows.append(
            (
                load(diag_hbm.at[t], tiles.at[first]),
                load(local_hbm.at[t], tiles.at[pl.ds(first + 1, KL)]),
            )
        )

    pl.semaphore_wait(barrier, len(everyone))
    ghost_copies = []
    for s in range(SLOTS):
        copy = pltpu.make_async_remote_copy(
            src_ref=ghost_hbm.at[0, pl.ds(s, 1)],
            dst_ref=ghosts.at[s],
            send_sem=ghost_send.at[s],
            recv_sem=ghost_recv.at[s],
            device_id=(around[s],),
            device_id_type=MESH,
        )
        copy.start()
        ghost_copies.append(copy)

    sub16 = lax.rem(lax.broadcasted_iota(jnp.int32, (2 * TD, TILE), 0), TD)
    sub8 = lax.broadcasted_iota(jnp.int32, (TD, TILE), 0)
    for t in range(TD):
        for k in range(KL):
            masks[KL * t + k] = jnp.where(sub16 == pattern[t, k], 1.0, 0.0).astype(BF16)

    load_rhs.wait()
    for t in range(TD):
        for c in range(COMP):
            krylov[0, t : t + 1, lanes(c)] = rhs[c : c + 1, lanes(t)]

    def spread_vector(j):
        for t in range(TD):
            row = jnp.broadcast_to(krylov[j, t : t + 1, :], (TD, WIDTH))
            spread[t] = halves(row)

    def send_couplings(j):
        copies = []
        for s in range(SLOTS):
            left = spread[rows[0, s]]
            both = jnp.dot(left, tiles[s], preferred_element_type=F32)
            term = both[:TD] + both[TD:]
            message = jnp.where(sub8 == 0, term[:, lanes(0)], 0.0)
            for c in range(1, COMP):
                message = jnp.where(sub8 == c, term[:, lanes(c)], message)
            if s < W:
                message = message * live[0, s].astype(F32)
            sent[j, s] = message
            copy = pltpu.make_async_remote_copy(
                src_ref=sent.at[j, s],
                dst_ref=got.at[j, s],
                send_sem=halo_send.at[j, s],
                recv_sem=halo_recv.at[j, s],
                device_id=(around[s],),
                device_id_type=MESH,
            )
            copy.start()
            copies.append(copy)
        return copies

    def multiply_own(j):
        total = None
        for t in range(TD):
            if j == 0:
                for copy in load_rows[t]:
                    copy.wait()
            vector = spread[t]
            for k in range(PER_ROW):
                if k == 0:
                    mask = jnp.where(sub16 == t, 1.0, 0.0).astype(BF16)
                else:
                    mask = masks[KL * t + k - 1]
                left = vector * jnp.concatenate([mask] * COMP, axis=1)
                part = jnp.dot(left, tiles[SLOTS + PER_ROW * t + k], preferred_element_type=F32)
                total = part if total is None else total + part
        return total[:TD] + total[TD:]

    def finish(j, own, copies):
        for copy in copies:
            copy.wait_recv()
        left = []
        for c in range(COMP):
            blocks = []
            for s in range(SLOTS):
                row = jnp.broadcast_to(got[j, s, c : c + 1, :], (TD, TILE))
                blocks.append(halves(row) * place[s])
            left.append(jnp.concatenate(blocks, axis=1))
        added = jnp.dot(jnp.concatenate(left, axis=0), pick[...], preferred_element_type=F32)
        for c in range(COMP):
            first = 2 * TD * c
            krylov[j + 1, :, lanes(c)] = (
                own[:, lanes(c)]
                + (added[first : first + TD] + added[first + TD : first + 2 * TD])
                - SHIFT * krylov[j, :, lanes(c)]
            )

    def pair_row(i, j):
        total = None
        for c in range(COMP):
            term = krylov[i, :, lanes(c)] * krylov[j, :, lanes(c)]
            total = term if total is None else total + term
        return jnp.sum(total, axis=0, keepdims=True)

    all_copies = list(ghost_copies)
    for j in range(ITERS):
        spread_vector(j)
        if j == 0:
            load_up.wait()
            load_down.wait()
        copies = send_couplings(j)
        all_copies.extend(copies)
        if j == 0:
            for s in range(SLOTS):
                ghost_copies[s].wait_recv()
                index = jnp.broadcast_to(ghosts[s], (TILE, TILE))
                sub = lax.broadcasted_iota(jnp.int32, (TILE, TILE), 0)
                chosen = jnp.where(jnp.bitwise_and(index, TILE - 1) == sub, 1.0, 0.0)
                pick[s * TILE : (s + 1) * TILE, :] = chosen.T.astype(BF16)
                row = jnp.broadcast_to(ghosts[s], (2 * TD, TILE))
                where = jnp.where(jnp.right_shift(row, 7) == sub16, 1.0, 0.0)
                if s >= W:
                    where = where * live[0, s - W].astype(F32)
                place[s] = where.astype(BF16)
        own = multiply_own(j)
        finish(j, own, copies)

    total = jnp.zeros((2 * TD, TILE), F32)
    sub = lax.broadcasted_iota(jnp.int32, (2 * TD, TILE), 0)
    for position, (i, j) in enumerate(PAIRS):
        total = jnp.where(sub == position, pair_row(i, j), total)
    part_a[...] = total
    stage_a = []
    for d in range(1, ROW):
        copy = pltpu.make_async_remote_copy(
            src_ref=part_a,
            dst_ref=recv_a.at[d - 1],
            send_sem=send_a.at[d - 1],
            recv_sem=got_a.at[d - 1],
            device_id=(peers_a[d - 1],),
            device_id_type=MESH,
        )
        copy.start()
        stage_a.append(copy)
    for j in range(1, ITERS):
        for t in range(TD):
            for c in range(COMP):
                nodes[j - 1, c : c + 1, lanes(t)] = krylov[j, t : t + 1, lanes(c)]
    for copy in stage_a:
        copy.wait_recv()
    for d in range(1, ROW):
        total = total + recv_a[d - 1]
    part_b[...] = total
    stage_b = []
    for d in range(1, columns):
        copy = pltpu.make_async_remote_copy(
            src_ref=part_b,
            dst_ref=recv_b.at[d - 1],
            send_sem=send_b.at[d - 1],
            recv_sem=got_b.at[d - 1],
            device_id=(peers_b[d - 1],),
            device_id_type=MESH,
        )
        copy.start()
        stage_b.append(copy)
    for copy in stage_b:
        copy.wait_recv()
    for d in range(1, columns):
        total = total + recv_b[d - 1]
    sums = jnp.sum(total, axis=1, keepdims=True)
    gram = {
        pair: jnp.broadcast_to(sums[position : position + 1, :], (TD, TILE))
        for position, pair in enumerate(PAIRS)
    }
    weights = [weight[:COMP] for weight in small_solve(gram)]
    for t in range(TD):
        value = weights[0] * rhs[:, lanes(t)]
        for j in range(1, ITERS):
            value = value + weights[j] * nodes[j - 1, :, lanes(t)]
        out_ref[:, lanes(t)] = value
    for copy in all_copies + stage_a + stage_b:
        copy.wait_send()


def local(n, *arrays):
    anywhere = pl.BlockSpec(memory_space=pl.ANY)
    scalars = pl.BlockSpec(memory_space=pltpu.SMEM)
    vmem = pltpu.VMEM
    dma = pltpu.SemaphoreType.DMA
    columns = n // ROW
    rhs = arrays[0]
    return pl.pallas_call(
        functools.partial(kernel, n),
        out_shape=jax.ShapeDtypeStruct(rhs.shape, F32),
        in_specs=[anywhere] * 5 + [scalars] * 2 + [anywhere, scalars],
        out_specs=pl.BlockSpec(memory_space=pltpu.VMEM),
        scratch_shapes=[
            vmem((SLOTS + PER_ROW * TD, WIDTH, WIDTH), BF16),
            vmem(rhs.shape, F32),
            vmem((ITERS + 1, TD, WIDTH), F32),
            vmem((ITERS - 1,) + rhs.shape, F32),
            vmem((TD, 2 * TD, WIDTH), BF16),
            vmem((TD * KL, 2 * TD, TILE), BF16),
            vmem((SLOTS, 1, TILE), jnp.int32),
            vmem((SLOTS * TILE, TILE), BF16),
            vmem((SLOTS, 2 * TD, TILE), BF16),
            vmem((ITERS, SLOTS, TD, TILE), F32),
            vmem((ITERS, SLOTS, TD, TILE), F32),
            vmem((2 * TD, TILE), F32),
            vmem((2 * TD, TILE), F32),
            vmem((ROW - 1, 2 * TD, TILE), F32),
            vmem((columns - 1, 2 * TD, TILE), F32),
            dma((3 + 2 * TD,)),
            dma((SLOTS,)),
            dma((SLOTS,)),
            dma((ITERS, SLOTS)),
            dma((ITERS, SLOTS)),
            dma((ROW - 1,)),
            dma((ROW - 1,)),
            dma((columns - 1,)),
            dma((columns - 1,)),
        ],
        compiler_params=pltpu.CompilerParams(
            collective_id=0, has_side_effects=True, vmem_limit_bytes=48 << 20
        ),
    )(*arrays)


def solution(mesh):
    in_specs = (
        P(None, "parts"),
        P("parts", None, None),
        P("parts", None, None, None),
        P("parts", None, None),
        P("parts", None, None),
        P("parts", None),
        P("parts", None),
        P("parts", None, None),
        P("parts", None),
    )
    return jax.shard_map(
        functools.partial(local, mesh.shape["parts"]),
        mesh=mesh,
        in_specs=in_specs,
        out_specs=P(None, "parts"),
        check_vma=False,
    )
```

time: 951 us -> 46 us (0.05); the launches traced: 940 us -> 45.8 us
  blocking collectives: 653 us -> 0 us
  other arithmetic: 84.2 us -> 0 us
  starting transfers between devices: 77.8 us -> 0 us
  waiting for transfers between devices: 52 us -> 0 us
  Pallas kernels: 0 us -> 38.9 us
  matrix products: 25.4 us -> 0 us
  local copies, waits for them, and re-layouts: 28.8 us -> 6.89 us
  between operations: 18.7 us -> 0.02 us
    psum x10 -> x0, blocking collectives: 653 us -> none  [the longest x6 396 us: local(): coeff = lax.psum(jnp.sum(vector * basis[i]), 'parts')]
    ppermute x33 -> x0, starting transfers between devices: 77.8 us -> none  [from_behind(): return lax.ppermute(value, axis, pairs)]
    scatter-add x18 -> x0, other arithmetic: 55 us -> none  [the longest x9 27.7 us: local(): result.at[:, ghost_down_in[apply_slot]].add(term_down.reshape(COMP, TILE))]
    ppermute x33 -> x0, waiting for transfers between devices: 52 us -> none  [from_behind(): return lax.ppermute(value, axis, pairs)]
    pallas_call x0 -> x1, Pallas kernels: none -> 38.9 us  [local(): pl.pallas_call(functools.partial(kernel, n), out_shape=jax.ShapeDtypeStru...]
    dot_general x28 -> x0, matrix products: 25.1 us -> none  [the longest x3 19.3 us: local(): jnp.einsum('tr,tkrc->tkc', tiles, local_tiles, preferred_element_type=jnp...]
    reduce_sum x10 -> x0, other arithmetic: 12.3 us -> none  [the longest x6 6.5 us: local(): coeff = lax.psum(jnp.sum(vector * basis[i]), 'parts')]
  transfers between devices with their start and end apart: 33 -> 0, of which waited for: 10 -> 0; matrix products, arithmetic and copies ran while one was open for 4% -> 0% of each run, Pallas kernels for 0% -> 0%
where the time goes in v1:
time: 46 us; the launch traced here: 45.8 us
  Pallas kernels  38.9 us (85%)
  local copies, waits for them, and re-layouts  6.89 us (15%)
    pallas_call x1, Pallas kernels, local(): pl.pallas_call(functools.partial(kernel, n), out_shape=jax.ShapeDtypeStru...  38.9 us
    unnamed x13, local copies, waits for them, and re-layouts  6.89 us

profile of v1, /device:TPU:1, one launch (start us, length us, event | category | flops | bytes accessed | tf_op | source)
XLA Modules:
  0.0 45.8 jit_solution(633807637948231158)
XLA Ops:
  0.0 0.8 %copy.10.pattern = s32[8,3]{1,0:T(8,128)S(1)} copy(s32[8,3]{0,1:T(4,128)} %param.14) | data formatting | bytes 192 | tf_op args[5]
  0.8 0.7 %copy.11.ghost_hbm = s32[1,6,128]{2,1,0:T(8,128)S(1)} copy(s32[1,6,128]{2,0,1:T(1,128)} %param.16) | data formatting | bytes 6144 | tf_op args[7]
  1.4 0.0 copy-start
  1.4 1.4 %copy-done = bf16[3,512,512]{2,1,0:T(8,128)(2,1)S(1)} copy-done((bf16[3,512,512]{2,1,0:T(8,128)(2,1)S(1)}, bf16[3,512,512]{2,1,0:T(8,128)(2,1)}, u32[]{:S(2)}) %copy-start) | copy-done | bytes 1572888
  2.9 0.0 copy-start.1
  2.9 1.4 %copy-done.1 = bf16[3,512,512]{2,1,0:T(8,128)(2,1)S(1)} copy-done((bf16[3,512,512]{2,1,0:T(8,128)(2,1)S(1)}, bf16[3,512,512]{2,1,0:T(8,128)(2,1)}, u32[]{:S(2)}) %copy-start.1) | copy-done | bytes 1572888
  4.3 0.0 copy-start.2
  4.3 0.7 %copy-done.2 = f32[4,1024]{1,0:T(4,128)S(1)} copy-done((f32[4,1024]{1,0:T(4,128)S(1)}, f32[4,1024]{1,0:T(4,128)}, u32[]{:S(2)}) %copy-start.2) | copy-done | bytes 16408
  5.0 0.0 copy-start.3
  5.0 0.7 %copy-done.3 = s32[1,6]{1,0:T(1,128)S(1)} copy-done((s32[1,6]{1,0:T(1,128)S(1)}, s32[1,6]{1,0:T(1,128)}, u32[]{:S(2)}) %copy-start.3) | copy-done | bytes 48
  5.6 0.0 copy-start.4
  5.6 0.7 %copy-done.4 = s32[1,3]{1,0:T(1,128)S(1)} copy-done((s32[1,3]{1,0:T(1,128)S(1)}, s32[1,3]{1,0:T(1,128)}, u32[]{:S(2)}) %copy-start.4) | copy-done | bytes 36
  6.3 38.9 %shard_map.91 = f32[4,1024]{1,0:T(4,128)S(1)} custom-call(f32[4,1024]{1,0:T(4,128)S(1)} %copy-done.2, bf16[8,512,512]{2,1,0:T(8,128)(2,1)} %diag_hbm.1, bf16[8,3,512,512]{3,2,1,0:T(8,128)(2,1)} %local_hbm.1, bf16[3,512,512]{2,1,0:T(8,128)(2,1)S(1)} %copy-done, bf16[3,512,512]{2,1,0:T(8,128)(2,1)S(1)} %copy-done.1, s32[8,3]{1,0:T(8,128)S(1)} %copy.10.pattern, ...), custom_call_target="tpu_custom_call" | custom-call | tf_op jit(solution)/shard_map/pallas_call | solution.py:361
  45.2 0.6 %copy.13 = f32[4,1024]{1,0:T(4,128)} copy(f32[4,1024]{1,0:T(4,128)S(1)} %shard_map.91) | data formatting | bytes 32768
Async XLA Ops:
  1.4 1.4 %copy-start = (bf16[3,512,512]{2,1,0:T(8,128)(2,1)S(1)}, bf16[3,512,512]{2,1,0:T(8,128)(2,1)}, u32[]{:S(2)}) copy-start(bf16[3,512,512]{2,1,0:T(8,128)(2,1)} %up_hbm.1) | copy-start | bytes 4718596
  2.9 1.4 %copy-start.1 = (bf16[3,512,512]{2,1,0:T(8,128)(2,1)S(1)}, bf16[3,512,512]{2,1,0:T(8,128)(2,1)}, u32[]{:S(2)}) copy-start(bf16[3,512,512]{2,1,0:T(8,128)(2,1)} %down_hbm.1) | copy-start | bytes 4718596
  4.3 0.7 %copy-start.2 = (f32[4,1024]{1,0:T(4,128)S(1)}, f32[4,1024]{1,0:T(4,128)}, u32[]{:S(2)}) copy-start(f32[4,1024]{1,0:T(4,128)} %rhs_hbm.1) | copy-start | bytes 49156
  5.0 0.7 %copy-start.3 = (s32[1,6]{1,0:T(1,128)S(1)}, s32[1,6]{1,0:T(1,128)}, u32[]{:S(2)}) copy-start(s32[1,6]{1,0:T(1,128)} %rows.1) | copy-start | bytes 76
  5.6 0.7 %copy-start.4 = (s32[1,3]{1,0:T(1,128)S(1)}, s32[1,3]{1,0:T(1,128)}, u32[]{:S(2)}) copy-start(s32[1,3]{1,0:T(1,128)} %live.1) | copy-start | bytes 40

commit v2 on v1

--- a/solution.py
+++ b/solution.py
@@ -1,4 +1,5 @@
 import functools
+import itertools
 
 import jax
 import jax.numpy as jnp
@@ -18,10 +19,13 @@
 PER_ROW = KL + 1
 SHIFT = 2.0
 EPS = 1e-06
-ROW = 8
 MESH = pl.DeviceIdType.MESH
 F32 = jnp.float32
 BF16 = jnp.bfloat16
+SIDE = 4
+OFFSETS = sorted(
+    itertools.product(range(SIDE), repeat=3), key=lambda d: -sum(min(k, SIDE - k) for k in d)
+)[:-1]
 PAIRS = [(i, j) for i in range(ITERS + 1) for j in range(i, ITERS + 1)]
 
 
@@ -109,11 +113,14 @@
     local_hbm,
     up_hbm,
     down_hbm,
+    pattern_hbm,
+    rows_hbm,
+    ghost_hbm,
+    live_hbm,
+    out_ref,
     pattern,
     rows,
-    ghost_hbm,
     live,
-    out_ref,
     tiles,
     rhs,
     krylov,
@@ -126,7 +133,6 @@
     sent,
     got,
     part_a,
-    part_b,
     recv_a,
     recv_b,
     load_sem,
@@ -140,18 +146,16 @@
     got_b,
 ):
     me = lax.axis_index("parts")
-    columns = n // ROW
-    place_in_row = lax.rem(me, ROW)
-    base = me - place_in_row
     around = [lax.rem(me + s + 1, n) for s in range(W)] + [
         lax.rem(me + n - s - 1, n) for s in range(W)
     ]
-    peers_a = [base + lax.rem(place_in_row + d, ROW) for d in range(1, ROW)]
-    peers_b = [lax.rem(me + d * ROW, n) for d in range(1, columns)]
-    everyone = around + peers_a + peers_b
-    barrier = pltpu.get_barrier_semaphore()
-    for other in everyone:
-        pl.semaphore_signal(barrier, inc=1, device_id=(other,), device_id_type=MESH)
+    core = lax.rem(me, 2)
+    digits = [lax.rem(me // 2, SIDE), lax.rem(me // (2 * SIDE), SIDE), me // (2 * SIDE * SIDE)]
+    moved = [
+        [2 * SIDE**axis * lax.rem(digits[axis] + d, SIDE) for d in range(SIDE)] for axis in range(3)
+    ]
+    partner = me + 1 - 2 * core
+    chips = [core + moved[0][dx] + moved[1][dz] + moved[2][dy] for dx, dz, dy in OFFSETS]
 
     loads = []
 
@@ -162,6 +166,7 @@
         return copy
 
     load_rhs = load(rhs_hbm, rhs)
+    load_small = [load(rows_hbm, rows), load(live_hbm, live), load(pattern_hbm, pattern)]
     load_up = load(up_hbm, tiles.at[pl.ds(0, W)])
     load_down = load(down_hbm, tiles.at[pl.ds(W, W)])
     load_rows = []
@@ -174,11 +179,16 @@
             )
         )
 
+    everyone = around + [partner] + chips
+    barrier = pltpu.get_barrier_semaphore()
+    for other in everyone:
+        pl.semaphore_signal(barrier, inc=1, device_id=(other,), device_id_type=MESH)
+
     pl.semaphore_wait(barrier, len(everyone))
     ghost_copies = []
     for s in range(SLOTS):
         copy = pltpu.make_async_remote_copy(
-            src_ref=ghost_hbm.at[0, pl.ds(s, 1)],
+            src_ref=ghost_hbm.at[s],
             dst_ref=ghosts.at[s],
             send_sem=ghost_send.at[s],
             recv_sem=ghost_recv.at[s],
@@ -188,11 +198,13 @@
         copy.start()
         ghost_copies.append(copy)
 
+    for copy in load_small:
+        copy.wait()
     sub16 = lax.rem(lax.broadcasted_iota(jnp.int32, (2 * TD, TILE), 0), TD)
     sub8 = lax.broadcasted_iota(jnp.int32, (TD, TILE), 0)
     for t in range(TD):
         for k in range(KL):
-            masks[KL * t + k] = jnp.where(sub16 == pattern[t, k], 1.0, 0.0).astype(BF16)
+            masks[KL * t + k] = jnp.where(sub16 == pattern[k, t], 1.0, 0.0).astype(BF16)
 
     load_rhs.wait()
     for t in range(TD):
@@ -294,51 +306,44 @@
         own = multiply_own(j)
         finish(j, own, copies)
 
+    sub = lax.broadcasted_iota(jnp.int32, (2 * TD, TILE), 0)
+    lane = lax.broadcasted_iota(jnp.int32, (2 * TD, TILE), 1)
     total = jnp.zeros((2 * TD, TILE), F32)
-    sub = lax.broadcasted_iota(jnp.int32, (2 * TD, TILE), 0)
     for position, (i, j) in enumerate(PAIRS):
         total = jnp.where(sub == position, pair_row(i, j), total)
-    part_a[...] = total
-    stage_a = []
-    for d in range(1, ROW):
-        copy = pltpu.make_async_remote_copy(
-            src_ref=part_a,
-            dst_ref=recv_a.at[d - 1],
-            send_sem=send_a.at[d - 1],
-            recv_sem=got_a.at[d - 1],
-            device_id=(peers_a[d - 1],),
+    total = jnp.where(lane == sub, jnp.sum(total, axis=1, keepdims=True), 0.0)
+    mine = jnp.sum(total, axis=0, keepdims=True)
+    part_a[...] = mine
+    other = pltpu.make_async_remote_copy(
+        src_ref=part_a,
+        dst_ref=recv_a,
+        send_sem=send_a,
+        recv_sem=got_a,
+        device_id=(partner,),
+        device_id_type=MESH,
+    )
+    other.start()
+    other.wait_recv()
+    last = len(OFFSETS)
+    recv_b[last : last + 1, :] = mine + recv_a[...]
+    for d in range(last):
+        pltpu.make_async_remote_copy(
+            src_ref=recv_b.at[pl.ds(last, 1)],
+            dst_ref=recv_b.at[pl.ds(d, 1)],
+            send_sem=send_b,
+            recv_sem=got_b,
+            device_id=(chips[d],),
             device_id_type=MESH,
-        )
-        copy.start()
-        stage_a.append(copy)
+        ).start()
     for j in range(1, ITERS):
         for t in range(TD):
             for c in range(COMP):
                 nodes[j - 1, c : c + 1, lanes(t)] = krylov[j, t : t + 1, lanes(c)]
-    for copy in stage_a:
-        copy.wait_recv()
-    for d in range(1, ROW):
-        total = total + recv_a[d - 1]
-    part_b[...] = total
-    stage_b = []
-    for d in range(1, columns):
-        copy = pltpu.make_async_remote_copy(
-            src_ref=part_b,
-            dst_ref=recv_b.at[d - 1],
-            send_sem=send_b.at[d - 1],
-            recv_sem=got_b.at[d - 1],
-            device_id=(peers_b[d - 1],),
-            device_id_type=MESH,
-        )
-        copy.start()
-        stage_b.append(copy)
-    for copy in stage_b:
-        copy.wait_recv()
-    for d in range(1, columns):
-        total = total + recv_b[d - 1]
-    sums = jnp.sum(total, axis=1, keepdims=True)
+    arrived = recv_b.at[pl.ds(0, last)]
+    pltpu.make_async_copy(arrived, arrived, got_b).wait()
+    sums = jnp.sum(recv_b[...], axis=0, keepdims=True)
     gram = {
-        pair: jnp.broadcast_to(sums[position : position + 1, :], (TD, TILE))
+        pair: jnp.broadcast_to(sums[:, position : position + 1], (TD, TILE))
         for position, pair in enumerate(PAIRS)
     }
     weights = [weight[:COMP] for weight in small_solve(gram)]
@@ -347,23 +352,26 @@
         for j in range(1, ITERS):
             value = value + weights[j] * nodes[j - 1, :, lanes(t)]
         out_ref[:, lanes(t)] = value
-    for copy in all_copies + stage_a + stage_b:
+    for copy in all_copies + [other]:
         copy.wait_send()
+    pltpu.make_async_copy(arrived, arrived, send_b).wait()
 
 
 def local(n, *arrays):
     anywhere = pl.BlockSpec(memory_space=pl.ANY)
-    scalars = pl.BlockSpec(memory_space=pltpu.SMEM)
+    smem = pltpu.SMEM
     vmem = pltpu.VMEM
     dma = pltpu.SemaphoreType.DMA
-    columns = n // ROW
     rhs = arrays[0]
     return pl.pallas_call(
         functools.partial(kernel, n),
         out_shape=jax.ShapeDtypeStruct(rhs.shape, F32),
-        in_specs=[anywhere] * 5 + [scalars] * 2 + [anywhere, scalars],
+        in_specs=[anywhere] * 9,
         out_specs=pl.BlockSpec(memory_space=pltpu.VMEM),
         scratch_shapes=[
+            smem((KL, TD), jnp.int32),
+            smem((1, SLOTS), jnp.int32),
+            smem((1, W), jnp.int32),
             vmem((SLOTS + PER_ROW * TD, WIDTH, WIDTH), BF16),
             vmem(rhs.shape, F32),
             vmem((ITERS + 1, TD, WIDTH), F32),
@@ -375,24 +383,23 @@
             vmem((SLOTS, 2 * TD, TILE), BF16),
             vmem((ITERS, SLOTS, TD, TILE), F32),
             vmem((ITERS, SLOTS, TD, TILE), F32),
-            vmem((2 * TD, TILE), F32),
-            vmem((2 * TD, TILE), F32),
-            vmem((ROW - 1, 2 * TD, TILE), F32),
-            vmem((columns - 1, 2 * TD, TILE), F32),
-            dma((3 + 2 * TD,)),
+            vmem((1, TILE), F32),
+            vmem((1, TILE), F32),
+            vmem((len(OFFSETS) + 1, TILE), F32),
+            dma((6 + 2 * TD,)),
             dma((SLOTS,)),
             dma((SLOTS,)),
             dma((ITERS, SLOTS)),
             dma((ITERS, SLOTS)),
-            dma((ROW - 1,)),
-            dma((ROW - 1,)),
-            dma((columns - 1,)),
-            dma((columns - 1,)),
+            dma,
+            dma,
+            dma,
+            dma,
         ],
         compiler_params=pltpu.CompilerParams(
-            collective_id=0, has_side_effects=True, vmem_limit_bytes=48 << 20
+            collective_id=0, has_side_effects=True, vmem_limit_bytes=65_000_000
         ),
-    )(*arrays)
+    )(*arrays[:5], arrays[5].T, arrays[6], jnp.swapaxes(arrays[7], 0, 1), arrays[8])
 
 
 def solution(mesh):

time: 46 us -> 39.4 us (0.86)
  local copies, waits for them, and re-layouts: 6.89 us -> 1.32 us
  Pallas kernels: 38.9 us -> 37.9 us
    unnamed x13 -> x1, local copies, waits for them, and re-layouts: 6.89 us -> 1.32 us
    pallas_call x1, Pallas kernels: 38.9 us -> 37.9 us  [local(): pl.pallas_call(functools.partial(kernel, n), out_shape=jax.ShapeDtypeStru...]
where the time goes in v2:
time: 39.4 us; the launch traced here: 39.3 us
  Pallas kernels  37.9 us (96%)
  local copies, waits for them, and re-layouts  1.32 us (3%)
    pallas_call x1, Pallas kernels, local(): pl.pallas_call(functools.partial(kernel, n), out_shape=jax.ShapeDtypeStru...  37.9 us
    unnamed x1, local copies, waits for them, and re-layouts  1.32 us

profile of v2, /device:TPU:1, one launch (start us, length us, event | category | flops | bytes accessed | tf_op | source)
XLA Modules:
  0.0 39.3 jit_solution(17224478907737018333)
XLA Ops:
  0.0 37.9 %shard_map.91 = f32[4,1024]{1,0:T(4,128)} custom-call(f32[4,1024]{1,0:T(4,128)} %rhs_hbm.1, bf16[8,512,512]{2,1,0:T(8,128)(2,1)} %diag_hbm.1, bf16[8,3,512,512]{3,2,1,0:T(8,128)(2,1)} %local_hbm.1, bf16[3,512,512]{2,1,0:T(8,128)(2,1)} %up_hbm.1, bf16[3,512,512]{2,1,0:T(8,128)(2,1)} %down_hbm.1, s32[3,8]{1,0:T(4,128)} %bitcast.3, s32[1,6]{1,0:T(1,128)} %rows_hbm.1, ...), custom_call_target="tpu_custom_call" | custom-call | tf_op jit(solution)/shard_map/pallas_call | solution.py:366
  37.9 1.3 %copy.11 = f32[4,1024]{1,0:T(4,128)} copy(f32[4,1024]{1,0:T(4,128)} %shard_map.91) | data formatting | bytes 32768

commit v3 on v2

--- a/solution.py
+++ b/solution.py
@@ -26,7 +26,11 @@
 OFFSETS = sorted(
     itertools.product(range(SIDE), repeat=3), key=lambda d: -sum(min(k, SIDE - k) for k in d)
 )[:-1]
-PAIRS = [(i, j) for i in range(ITERS + 1) for j in range(i, ITERS + 1)]
+LATE = {(i, ITERS): i for i in range(ITERS + 1)}
+EARLY = {
+    pair: TD + position
+    for position, pair in enumerate((i, j) for i in range(ITERS) for j in range(i, ITERS))
+}
 
 
 def lanes(c):
@@ -149,6 +153,9 @@
     around = [lax.rem(me + s + 1, n) for s in range(W)] + [
         lax.rem(me + n - s - 1, n) for s in range(W)
     ]
+    barrier = pltpu.get_barrier_semaphore()
+    for other in around:
+        pl.semaphore_signal(barrier, inc=1, device_id=(other,), device_id_type=MESH)
     core = lax.rem(me, 2)
     digits = [lax.rem(me // 2, SIDE), lax.rem(me // (2 * SIDE), SIDE), me // (2 * SIDE * SIDE)]
     moved = [
@@ -179,25 +186,8 @@
             )
         )
 
-    everyone = around + [partner] + chips
-    barrier = pltpu.get_barrier_semaphore()
-    for other in everyone:
+    for other in [partner] + chips:
         pl.semaphore_signal(barrier, inc=1, device_id=(other,), device_id_type=MESH)
-
-    pl.semaphore_wait(barrier, len(everyone))
-    ghost_copies = []
-    for s in range(SLOTS):
-        copy = pltpu.make_async_remote_copy(
-            src_ref=ghost_hbm.at[s],
-            dst_ref=ghosts.at[s],
-            send_sem=ghost_send.at[s],
-            recv_sem=ghost_recv.at[s],
-            device_id=(around[s],),
-            device_id_type=MESH,
-        )
-        copy.start()
-        ghost_copies.append(copy)
-
     for copy in load_small:
         copy.wait()
     sub16 = lax.rem(lax.broadcasted_iota(jnp.int32, (2 * TD, TILE), 0), TD)
@@ -216,29 +206,45 @@
             row = jnp.broadcast_to(krylov[j, t : t + 1, :], (TD, WIDTH))
             spread[t] = halves(row)
 
-    def send_couplings(j):
-        copies = []
-        for s in range(SLOTS):
+    far = 1 - lax.rem(me, 2 * SIDE) // SIDE
+    orders = []
+    for side in range(2):
+        down = far if side == 0 else 1 - far
+        for k in range(W):
+            target = lax.rem(me + n + (k + 1) * (1 - 2 * down), n)
+            orders.append((W * down + k, k, down, target))
+
+    def couple(j, chosen):
+        found = []
+        for s, k, down, target in chosen:
             left = spread[rows[0, s]]
-            both = jnp.dot(left, tiles[s], preferred_element_type=F32)
+            found.append(jnp.dot(left, tiles[s], preferred_element_type=F32))
+        for (s, k, down, target), both in zip(chosen, found):
             term = both[:TD] + both[TD:]
-            message = jnp.where(sub8 == 0, term[:, lanes(0)], 0.0)
+            message = term[:, lanes(0)]
             for c in range(1, COMP):
                 message = jnp.where(sub8 == c, term[:, lanes(c)], message)
-            if s < W:
-                message = message * live[0, s].astype(F32)
-            sent[j, s] = message
+            factor = (down + (1 - down) * live[0, k]).astype(F32)
+            sent[j, s] = (message * factor)[:COMP]
+
+    def send(j, chosen):
+        copies = []
+        for s, k, down, target in chosen:
             copy = pltpu.make_async_remote_copy(
                 src_ref=sent.at[j, s],
                 dst_ref=got.at[j, s],
                 send_sem=halo_send.at[j, s],
                 recv_sem=halo_recv.at[j, s],
-                device_id=(around[s],),
+                device_id=(target,),
                 device_id_type=MESH,
             )
             copy.start()
             copies.append(copy)
         return copies
+
+    def wait_halo(j):
+        for s in range(SLOTS):
+            pltpu.make_async_copy(got.at[j, s], got.at[j, s], halo_recv.at[j, s]).wait()
 
     def multiply_own(j):
         total = None
@@ -257,9 +263,8 @@
                 total = part if total is None else total + part
         return total[:TD] + total[TD:]
 
-    def finish(j, own, copies):
-        for copy in copies:
-            copy.wait_recv()
+    def finish(j, own):
+        wait_halo(j)
         left = []
         for c in range(COMP):
             blocks = []
@@ -283,19 +288,48 @@
             total = term if total is None else total + term
         return jnp.sum(total, axis=0, keepdims=True)
 
-    all_copies = list(ghost_copies)
+    lane8 = lax.broadcasted_iota(jnp.int32, (TD, TILE), 1)
+
+    def gather_pairs(pairs):
+        total = jnp.zeros((TD, TILE), F32)
+        first = min(pairs.values())
+        for (i, j), position in pairs.items():
+            total = jnp.where(sub8 == position - first, pair_row(i, j), total)
+        total = jnp.where(lane8 == sub8 + first, jnp.sum(total, axis=1, keepdims=True), 0.0)
+        return jnp.sum(total, axis=0, keepdims=True)
+
+    all_copies = []
     for j in range(ITERS):
         spread_vector(j)
         if j == 0:
             load_up.wait()
             load_down.wait()
-        copies = send_couplings(j)
-        all_copies.extend(copies)
+            couple(j, orders)
+            pl.semaphore_wait(barrier, SLOTS + 1 + len(chips))
+            ghost_copies = []
+            for s in range(SLOTS):
+                copy = pltpu.make_async_remote_copy(
+                    src_ref=ghost_hbm.at[s],
+                    dst_ref=ghosts.at[s],
+                    send_sem=ghost_send.at[s],
+                    recv_sem=ghost_recv.at[s],
+                    device_id=(around[s],),
+                    device_id_type=MESH,
+                )
+                copy.start()
+                ghost_copies.append(copy)
+            all_copies.extend(ghost_copies)
+            all_copies.extend(send(j, orders))
+        else:
+            for chosen in (orders[:W], orders[W:]):
+                couple(j, chosen)
+                all_copies.extend(send(j, chosen))
+        own = multiply_own(j)
         if j == 0:
+            sub = lax.broadcasted_iota(jnp.int32, (TILE, TILE), 0)
             for s in range(SLOTS):
                 ghost_copies[s].wait_recv()
                 index = jnp.broadcast_to(ghosts[s], (TILE, TILE))
-                sub = lax.broadcasted_iota(jnp.int32, (TILE, TILE), 0)
                 chosen = jnp.where(jnp.bitwise_and(index, TILE - 1) == sub, 1.0, 0.0)
                 pick[s * TILE : (s + 1) * TILE, :] = chosen.T.astype(BF16)
                 row = jnp.broadcast_to(ghosts[s], (2 * TD, TILE))
@@ -303,16 +337,10 @@
                 if s >= W:
                     where = where * live[0, s - W].astype(F32)
                 place[s] = where.astype(BF16)
-        own = multiply_own(j)
-        finish(j, own, copies)
-
-    sub = lax.broadcasted_iota(jnp.int32, (2 * TD, TILE), 0)
-    lane = lax.broadcasted_iota(jnp.int32, (2 * TD, TILE), 1)
-    total = jnp.zeros((2 * TD, TILE), F32)
-    for position, (i, j) in enumerate(PAIRS):
-        total = jnp.where(sub == position, pair_row(i, j), total)
-    total = jnp.where(lane == sub, jnp.sum(total, axis=1, keepdims=True), 0.0)
-    mine = jnp.sum(total, axis=0, keepdims=True)
+        if j + 1 == ITERS:
+            early = gather_pairs(EARLY)
+        finish(j, own)
+    mine = early + gather_pairs(LATE)
     part_a[...] = mine
     other = pltpu.make_async_remote_copy(
         src_ref=part_a,
@@ -344,7 +372,7 @@
     sums = jnp.sum(recv_b[...], axis=0, keepdims=True)
     gram = {
         pair: jnp.broadcast_to(sums[:, position : position + 1], (TD, TILE))
-        for position, pair in enumerate(PAIRS)
+        for pair, position in (EARLY | LATE).items()
     }
     weights = [weight[:COMP] for weight in small_solve(gram)]
     for t in range(TD):
@@ -365,7 +393,7 @@
     rhs = arrays[0]
     return pl.pallas_call(
         functools.partial(kernel, n),
-        out_shape=jax.ShapeDtypeStruct(rhs.shape, F32),
+        out_shape=pltpu.VMEM(rhs.shape, F32),
         in_specs=[anywhere] * 9,
         out_specs=pl.BlockSpec(memory_space=pltpu.VMEM),
         scratch_shapes=[
@@ -381,8 +409,8 @@
             vmem((SLOTS, 1, TILE), jnp.int32),
             vmem((SLOTS * TILE, TILE), BF16),
             vmem((SLOTS, 2 * TD, TILE), BF16),
-            vmem((ITERS, SLOTS, TD, TILE), F32),
-            vmem((ITERS, SLOTS, TD, TILE), F32),
+            vmem((ITERS, SLOTS, COMP, TILE), F32),
+            vmem((ITERS, SLOTS, COMP, TILE), F32),
             vmem((1, TILE), F32),
             vmem((1, TILE), F32),
             vmem((len(OFFSETS) + 1, TILE), F32),

time: 39.4 us -> 35 us (0.89)
  Pallas kernels: 37.9 us -> 34.3 us
  local copies, waits for them, and re-layouts: 1.32 us -> 0.61 us
    pallas_call x1, Pallas kernels: 37.9 us -> 34.3 us  [local(): pl.pallas_call(functools.partial(kernel, n), out_shape=pltpu.VMEM(rhs.sha...]
    unnamed x1, local copies, waits for them, and re-layouts: 1.32 us -> 0.61 us
where the time goes in v3:
time: 35 us; the launch traced here: 34.9 us
  Pallas kernels  34.3 us (98%)
  local copies, waits for them, and re-layouts  0.61 us (2%)
    pallas_call x1, Pallas kernels, local(): pl.pallas_call(functools.partial(kernel, n), out_shape=pltpu.VMEM(rhs.sha...  34.3 us

profile of v3, /device:TPU:1, one launch (start us, length us, event | category | flops | bytes accessed | tf_op | source)
XLA Modules:
  0.0 34.9 jit_solution(3173841346341458188)
XLA Ops:
  0.0 34.3 %shard_map.91 = f32[4,1024]{1,0:T(4,128)S(1)} custom-call(f32[4,1024]{1,0:T(4,128)} %rhs_hbm.1, bf16[8,512,512]{2,1,0:T(8,128)(2,1)} %diag_hbm.1, bf16[8,3,512,512]{3,2,1,0:T(8,128)(2,1)} %local_hbm.1, bf16[3,512,512]{2,1,0:T(8,128)(2,1)} %up_hbm.1, bf16[3,512,512]{2,1,0:T(8,128)(2,1)} %down_hbm.1, s32[3,8]{1,0:T(4,128)} %bitcast.3, s32[1,6]{1,0:T(1,128)} %rows_hbm.1, ...), custom_call_target="tpu_custom_call" | custom-call | tf_op jit(solution)/shard_map/pallas_call | solution.py:394
  34.3 0.6 %copy.11 = f32[4,1024]{1,0:T(4,128)} copy(f32[4,1024]{1,0:T(4,128)S(1)} %shard_map.91) | data formatting | bytes 32768

commit v4 on v3

--- a/solution.py
+++ b/solution.py
@@ -1,5 +1,4 @@
 import functools
-import itertools
 
 import jax
 import jax.numpy as jnp
@@ -23,9 +22,6 @@
 F32 = jnp.float32
 BF16 = jnp.bfloat16
 SIDE = 4
-OFFSETS = sorted(
-    itertools.product(range(SIDE), repeat=3), key=lambda d: -sum(min(k, SIDE - k) for k in d)
-)[:-1]
 LATE = {(i, ITERS): i for i in range(ITERS + 1)}
 EARLY = {
     pair: TD + position
@@ -136,33 +132,33 @@
     place,
     sent,
     got,
-    part_a,
-    recv_a,
-    recv_b,
+    recv,
     load_sem,
     ghost_send,
     ghost_recv,
     halo_send,
     halo_recv,
-    send_a,
-    got_a,
-    send_b,
-    got_b,
+    present,
+    all_send,
+    all_got,
 ):
     me = lax.axis_index("parts")
     around = [lax.rem(me + s + 1, n) for s in range(W)] + [
         lax.rem(me + n - s - 1, n) for s in range(W)
     ]
-    barrier = pltpu.get_barrier_semaphore()
-    for other in around:
-        pl.semaphore_signal(barrier, inc=1, device_id=(other,), device_id_type=MESH)
     core = lax.rem(me, 2)
     digits = [lax.rem(me // 2, SIDE), lax.rem(me // (2 * SIDE), SIDE), me // (2 * SIDE * SIDE)]
     moved = [
         [2 * SIDE**axis * lax.rem(digits[axis] + d, SIDE) for d in range(SIDE)] for axis in range(3)
     ]
+    lines = [
+        [me - moved[axis][0] + moved[axis][d] for d in range(1, SIDE)] for axis in range(3)
+    ]
+    greeted = around + lines[0] + lines[1] + lines[2]
+    barrier = pltpu.get_barrier_semaphore()
+    for other in greeted:
+        pl.semaphore_signal(barrier, inc=1, device_id=(other,), device_id_type=MESH)
     partner = me + 1 - 2 * core
-    chips = [core + moved[0][dx] + moved[1][dz] + moved[2][dy] for dx, dz, dy in OFFSETS]
 
     loads = []
 
@@ -186,8 +182,6 @@
             )
         )
 
-    for other in [partner] + chips:
-        pl.semaphore_signal(barrier, inc=1, device_id=(other,), device_id_type=MESH)
     for copy in load_small:
         copy.wait()
     sub16 = lax.rem(lax.broadcasted_iota(jnp.int32, (2 * TD, TILE), 0), TD)
@@ -305,71 +299,63 @@
             load_up.wait()
             load_down.wait()
             couple(j, orders)
-            pl.semaphore_wait(barrier, SLOTS + 1 + len(chips))
-            ghost_copies = []
-            for s in range(SLOTS):
-                copy = pltpu.make_async_remote_copy(
-                    src_ref=ghost_hbm.at[s],
-                    dst_ref=ghosts.at[s],
-                    send_sem=ghost_send.at[s],
-                    recv_sem=ghost_recv.at[s],
-                    device_id=(around[s],),
-                    device_id_type=MESH,
-                )
-                copy.start()
-                ghost_copies.append(copy)
-            all_copies.extend(ghost_copies)
-            all_copies.extend(send(j, orders))
+            pl.semaphore_wait(barrier, len(greeted))
+            for chosen in (orders[:W], orders[W:]):
+                for s, k, down, target in chosen:
+                    copy = pltpu.make_async_remote_copy(
+                        src_ref=ghost_hbm.at[s],
+                        dst_ref=ghosts.at[s],
+                        send_sem=ghost_send.at[s],
+                        recv_sem=ghost_recv.at[s],
+                        device_id=(target,),
+                        device_id_type=MESH,
+                    )
+                    copy.start()
+                    all_copies.append(copy)
+                all_copies.extend(send(j, chosen))
         else:
             for chosen in (orders[:W], orders[W:]):
                 couple(j, chosen)
                 all_copies.extend(send(j, chosen))
+        others = [lines[1], lines[2], [partner]][j]
+        for other in others:
+            pl.semaphore_signal(
+                present.at[j], inc=1, device_id=(other,), device_id_type=MESH
+            )
         own = multiply_own(j)
+        pl.semaphore_wait(present.at[j], len(others))
         if j == 0:
             sub = lax.broadcasted_iota(jnp.int32, (TILE, TILE), 0)
-            for s in range(SLOTS):
-                ghost_copies[s].wait_recv()
+            for s, k, down, target in orders:
+                pltpu.make_async_copy(ghosts.at[s], ghosts.at[s], ghost_recv.at[s]).wait()
                 index = jnp.broadcast_to(ghosts[s], (TILE, TILE))
-                chosen = jnp.where(jnp.bitwise_and(index, TILE - 1) == sub, 1.0, 0.0)
-                pick[s * TILE : (s + 1) * TILE, :] = chosen.T.astype(BF16)
+                hit = jnp.where(jnp.bitwise_and(index, TILE - 1) == sub, 1.0, 0.0)
+                pick[pl.ds(pl.multiple_of(s * TILE, TILE), TILE), :] = hit.T.astype(BF16)
                 row = jnp.broadcast_to(ghosts[s], (2 * TD, TILE))
-                where = jnp.where(jnp.right_shift(row, 7) == sub16, 1.0, 0.0)
-                if s >= W:
-                    where = where * live[0, s - W].astype(F32)
-                place[s] = where.astype(BF16)
+                hit = jnp.where(jnp.right_shift(row, 7) == sub16, 1.0, 0.0)
+                place[s] = (hit * (1 - down + down * live[0, k]).astype(F32)).astype(BF16)
         if j + 1 == ITERS:
             early = gather_pairs(EARLY)
         finish(j, own)
     mine = early + gather_pairs(LATE)
-    part_a[...] = mine
-    other = pltpu.make_async_remote_copy(
-        src_ref=part_a,
-        dst_ref=recv_a,
-        send_sem=send_a,
-        recv_sem=got_a,
-        device_id=(partner,),
-        device_id_type=MESH,
-    )
-    other.start()
-    other.wait_recv()
-    last = len(OFFSETS)
-    recv_b[last : last + 1, :] = mine + recv_a[...]
-    for d in range(last):
+    recv[pl.ds(me, 1), :] = mine
+    for d in range(n - 1):
+        target = d + jnp.minimum(jnp.maximum(d + 1 - me, 0), 1)
         pltpu.make_async_remote_copy(
-            src_ref=recv_b.at[pl.ds(last, 1)],
-            dst_ref=recv_b.at[pl.ds(d, 1)],
-            send_sem=send_b,
-            recv_sem=got_b,
-            device_id=(chips[d],),
+            src_ref=recv.at[pl.ds(me, 1)],
+            dst_ref=recv.at[pl.ds(me, 1)],
+            send_sem=all_send,
+            recv_sem=all_got,
+            device_id=(target,),
             device_id_type=MESH,
         ).start()
     for j in range(1, ITERS):
         for t in range(TD):
             for c in range(COMP):
                 nodes[j - 1, c : c + 1, lanes(t)] = krylov[j, t : t + 1, lanes(c)]
-    arrived = recv_b.at[pl.ds(0, last)]
-    pltpu.make_async_copy(arrived, arrived, got_b).wait()
-    sums = jnp.sum(recv_b[...], axis=0, keepdims=True)
+    arrived = recv.at[pl.ds(0, n - 1)]
+    pltpu.make_async_copy(arrived, arrived, all_got).wait()
+    sums = jnp.sum(recv[...], axis=0, keepdims=True)
     gram = {
         pair: jnp.broadcast_to(sums[:, position : position + 1], (TD, TILE))
         for pair, position in (EARLY | LATE).items()
@@ -380,9 +366,9 @@
         for j in range(1, ITERS):
             value = value + weights[j] * nodes[j - 1, :, lanes(t)]
         out_ref[:, lanes(t)] = value
-    for copy in all_copies + [other]:
+    for copy in all_copies:
         copy.wait_send()
-    pltpu.make_async_copy(arrived, arrived, send_b).wait()
+    pltpu.make_async_copy(arrived, arrived, all_send).wait()
 
 
 def local(n, *arrays):
@@ -411,16 +397,13 @@
             vmem((SLOTS, 2 * TD, TILE), BF16),
             vmem((ITERS, SLOTS, COMP, TILE), F32),
             vmem((ITERS, SLOTS, COMP, TILE), F32),
-            vmem((1, TILE), F32),
-            vmem((1, TILE), F32),
-            vmem((len(OFFSETS) + 1, TILE), F32),
+            vmem((n, TILE), F32),
             dma((6 + 2 * TD,)),
             dma((SLOTS,)),
             dma((SLOTS,)),
             dma((ITERS, SLOTS)),
             dma((ITERS, SLOTS)),
-            dma,
-            dma,
+            pltpu.SemaphoreType.REGULAR((ITERS,)),
             dma,
             dma,
         ],

time: 35 us -> 34 us (0.971)
  Pallas kernels: 34.3 us -> 33.2 us
    pallas_call x1, Pallas kernels: 34.3 us -> 33.2 us  [local(): pl.pallas_call(functools.partial(kernel, n), out_shape=pltpu.VMEM(rhs.sha...]
where the time goes in v4:
time: 34 us; the launch traced here: 33.9 us
  Pallas kernels  33.2 us (98%)
  local copies, waits for them, and re-layouts  0.61 us (2%)
    pallas_call x1, Pallas kernels, local(): pl.pallas_call(functools.partial(kernel, n), out_shape=pltpu.VMEM(rhs.sha...  33.2 us

profile of v4, /device:TPU:1, one launch (start us, length us, event | category | flops | bytes accessed | tf_op | source)
XLA Modules:
  0.0 33.9 jit_solution(15762219410574178541)
XLA Ops:
  0.0 33.2 %shard_map.91 = f32[4,1024]{1,0:T(4,128)S(1)} custom-call(f32[4,1024]{1,0:T(4,128)} %rhs_hbm.1, bf16[8,512,512]{2,1,0:T(8,128)(2,1)} %diag_hbm.1, bf16[8,3,512,512]{3,2,1,0:T(8,128)(2,1)} %local_hbm.1, bf16[3,512,512]{2,1,0:T(8,128)(2,1)} %up_hbm.1, bf16[3,512,512]{2,1,0:T(8,128)(2,1)} %down_hbm.1, s32[3,8]{1,0:T(4,128)} %bitcast.3, s32[1,6]{1,0:T(1,128)} %rows_hbm.1, ...), custom_call_target="tpu_custom_call" | custom-call | tf_op jit(solution)/shard_map/pallas_call | solution.py:380
  33.3 0.6 %copy.11 = f32[4,1024]{1,0:T(4,128)} copy(f32[4,1024]{1,0:T(4,128)S(1)} %shard_map.91) | data formatting | bytes 32768

commit v5 on v4

--- a/solution.py
+++ b/solution.py
@@ -18,6 +18,7 @@
 PER_ROW = KL + 1
 SHIFT = 2.0
 EPS = 1e-06
+LAG = 2
 MESH = pl.DeviceIdType.MESH
 F32 = jnp.float32
 BF16 = jnp.bfloat16
@@ -200,41 +201,40 @@
             row = jnp.broadcast_to(krylov[j, t : t + 1, :], (TD, WIDTH))
             spread[t] = halves(row)
 
+    all_copies = []
     far = 1 - lax.rem(me, 2 * SIDE) // SIDE
     orders = []
     for side in range(2):
         down = far if side == 0 else 1 - far
-        for k in range(W):
+        for k in reversed(range(W)):
             target = lax.rem(me + n + (k + 1) * (1 - 2 * down), n)
             orders.append((W * down + k, k, down, target))
 
-    def couple(j, chosen):
-        found = []
-        for s, k, down, target in chosen:
-            left = spread[rows[0, s]]
-            found.append(jnp.dot(left, tiles[s], preferred_element_type=F32))
-        for (s, k, down, target), both in zip(chosen, found):
-            term = both[:TD] + both[TD:]
-            message = term[:, lanes(0)]
-            for c in range(1, COMP):
-                message = jnp.where(sub8 == c, term[:, lanes(c)], message)
-            factor = (down + (1 - down) * live[0, k]).astype(F32)
-            sent[j, s] = (message * factor)[:COMP]
-
-    def send(j, chosen):
-        copies = []
-        for s, k, down, target in chosen:
-            copy = pltpu.make_async_remote_copy(
-                src_ref=sent.at[j, s],
-                dst_ref=got.at[j, s],
-                send_sem=halo_send.at[j, s],
-                recv_sem=halo_recv.at[j, s],
-                device_id=(target,),
-                device_id_type=MESH,
-            )
-            copy.start()
-            copies.append(copy)
-        return copies
+    def product(order):
+        s = order[0]
+        return jnp.dot(spread[rows[0, s]], tiles[s], preferred_element_type=F32)
+
+    def keep(j, order, both):
+        s, k, down, target = order
+        term = both[:TD] + both[TD:]
+        message = term[:, lanes(0)]
+        for c in range(1, COMP):
+            message = jnp.where(sub8 == c, term[:, lanes(c)], message)
+        factor = (down + (1 - down) * live[0, k]).astype(F32)
+        sent[j, s] = (message * factor)[:COMP]
+
+    def send(j, order):
+        s, k, down, target = order
+        copy = pltpu.make_async_remote_copy(
+            src_ref=sent.at[j, s],
+            dst_ref=got.at[j, s],
+            send_sem=halo_send.at[j, s],
+            recv_sem=halo_recv.at[j, s],
+            device_id=(target,),
+            device_id_type=MESH,
+        )
+        copy.start()
+        all_copies.append(copy)
 
     def wait_halo(j):
         for s in range(SLOTS):
@@ -292,13 +292,14 @@
         total = jnp.where(lane8 == sub8 + first, jnp.sum(total, axis=1, keepdims=True), 0.0)
         return jnp.sum(total, axis=0, keepdims=True)
 
-    all_copies = []
     for j in range(ITERS):
         spread_vector(j)
         if j == 0:
             load_up.wait()
             load_down.wait()
-            couple(j, orders)
+            found = [product(order) for order in orders]
+            for order, both in zip(orders, found):
+                keep(j, order, both)
             pl.semaphore_wait(barrier, len(greeted))
             for chosen in (orders[:W], orders[W:]):
                 for s, k, down, target in chosen:
@@ -312,11 +313,16 @@
                     )
                     copy.start()
                     all_copies.append(copy)
-                all_copies.extend(send(j, chosen))
+                for order in chosen:
+                    send(j, order)
         else:
-            for chosen in (orders[:W], orders[W:]):
-                couple(j, chosen)
-                all_copies.extend(send(j, chosen))
+            found = []
+            for position in range(SLOTS + LAG):
+                if position < SLOTS:
+                    found.append(product(orders[position]))
+                if position >= LAG:
+                    keep(j, orders[position - LAG], found[position - LAG])
+                    send(j, orders[position - LAG])
         others = [lines[1], lines[2], [partner]][j]
         for other in others:
             pl.semaphore_signal(

time: 34 us -> 33.8 us (level)
  no operation moved by 1% of the time
where the time goes in v5:
time: 33.8 us; the launch traced here: 33.7 us
  Pallas kernels  33.1 us (98%)
  local copies, waits for them, and re-layouts  0.61 us (2%)
    pallas_call x1, Pallas kernels, local(): pl.pallas_call(functools.partial(kernel, n), out_shape=pltpu.VMEM(rhs.sha...  33.1 us

profile of v5, /device:TPU:1, one launch (start us, length us, event | category | flops | bytes accessed | tf_op | source)
XLA Modules:
  0.0 33.7 jit_solution(8207510626969444739)
XLA Ops:
  0.0 33.1 %shard_map.91 = f32[4,1024]{1,0:T(4,128)S(1)} custom-call(f32[4,1024]{1,0:T(4,128)} %rhs_hbm.1, bf16[8,512,512]{2,1,0:T(8,128)(2,1)} %diag_hbm.1, bf16[8,3,512,512]{3,2,1,0:T(8,128)(2,1)} %local_hbm.1, bf16[3,512,512]{2,1,0:T(8,128)(2,1)} %up_hbm.1, bf16[3,512,512]{2,1,0:T(8,128)(2,1)} %down_hbm.1, s32[3,8]{1,0:T(4,128)} %bitcast.3, s32[1,6]{1,0:T(1,128)} %rows_hbm.1, ...), custom_call_target="tpu_custom_call" | custom-call | tf_op jit(solution)/shard_map/pallas_call | solution.py:386
  33.1 0.6 %copy.11 = f32[4,1024]{1,0:T(4,128)} copy(f32[4,1024]{1,0:T(4,128)S(1)} %shard_map.91) | data formatting | bytes 32768

commit v6 on v5

--- a/solution.py
+++ b/solution.py
@@ -275,21 +275,19 @@
                 - SHIFT * krylov[j, :, lanes(c)]
             )
 
-    def pair_row(i, j):
+    def pair_lanes(i, j):
         total = None
         for c in range(COMP):
             term = krylov[i, :, lanes(c)] * krylov[j, :, lanes(c)]
             total = term if total is None else total + term
-        return jnp.sum(total, axis=0, keepdims=True)
+        return jnp.sum(total, axis=1, keepdims=True)
 
     lane8 = lax.broadcasted_iota(jnp.int32, (TD, TILE), 1)
 
     def gather_pairs(pairs):
         total = jnp.zeros((TD, TILE), F32)
-        first = min(pairs.values())
         for (i, j), position in pairs.items():
-            total = jnp.where(sub8 == position - first, pair_row(i, j), total)
-        total = jnp.where(lane8 == sub8 + first, jnp.sum(total, axis=1, keepdims=True), 0.0)
+            total = jnp.where(lane8 == position, pair_lanes(i, j), total)
         return jnp.sum(total, axis=0, keepdims=True)
 
     for j in range(ITERS):
@@ -301,20 +299,19 @@
             for order, both in zip(orders, found):
                 keep(j, order, both)
             pl.semaphore_wait(barrier, len(greeted))
-            for chosen in (orders[:W], orders[W:]):
-                for s, k, down, target in chosen:
-                    copy = pltpu.make_async_remote_copy(
-                        src_ref=ghost_hbm.at[s],
-                        dst_ref=ghosts.at[s],
-                        send_sem=ghost_send.at[s],
-                        recv_sem=ghost_recv.at[s],
-                        device_id=(target,),
-                        device_id_type=MESH,
-                    )
-                    copy.start()
-                    all_copies.append(copy)
-                for order in chosen:
-                    send(j, order)
+            for order in orders:
+                send(j, order)
+            for s, k, down, target in orders:
+                copy = pltpu.make_async_remote_copy(
+                    src_ref=ghost_hbm.at[s],
+                    dst_ref=ghosts.at[s],
+                    send_sem=ghost_send.at[s],
+                    recv_sem=ghost_recv.at[s],
+                    device_id=(target,),
+                    device_id_type=MESH,
+                )
+                copy.start()
+                all_copies.append(copy)
         else:
             found = []
             for position in range(SLOTS + LAG):

time: 33.8 us -> 33.8 us (level)
  no operation moved by 1% of the time
where the time goes in v6:
time: 33.8 us; the launch traced here: 33.7 us
  Pallas kernels  33.1 us (98%)
  local copies, waits for them, and re-layouts  0.61 us (2%)
    pallas_call x1, Pallas kernels, local(): pl.pallas_call(functools.partial(kernel, n), out_shape=pltpu.VMEM(rhs.sha...  33.1 us

profile of v6, /device:TPU:1, one launch (start us, length us, event | category | flops | bytes accessed | tf_op | source)
XLA Modules:
  0.0 33.7 jit_solution(11744804209501245680)
XLA Ops:
  0.0 33.1 %shard_map.91 = f32[4,1024]{1,0:T(4,128)S(1)} custom-call(f32[4,1024]{1,0:T(4,128)} %rhs_hbm.1, bf16[8,512,512]{2,1,0:T(8,128)(2,1)} %diag_hbm.1, bf16[8,3,512,512]{3,2,1,0:T(8,128)(2,1)} %local_hbm.1, bf16[3,512,512]{2,1,0:T(8,128)(2,1)} %up_hbm.1, bf16[3,512,512]{2,1,0:T(8,128)(2,1)} %down_hbm.1, s32[3,8]{1,0:T(4,128)} %bitcast.3, s32[1,6]{1,0:T(1,128)} %rows_hbm.1, ...), custom_call_target="tpu_custom_call" | custom-call | tf_op jit(solution)/shard_map/pallas_call | solution.py:383
  33.1 0.6 %copy.11 = f32[4,1024]{1,0:T(4,128)} copy(f32[4,1024]{1,0:T(4,128)S(1)} %shard_map.91) | data formatting | bytes 32768
